TPU v7x, 128 devices: a whole 4x4x4 slice. The times are simulated.
128 devices in a mesh: seq: 8 (over z, y_hi), chan: 8 (over x, core), dp: 2 (over y_lo).
Axes of the slice: x: 4, y: 4 (y_hi: 2, y_lo: 2; y = y_hi * 2 + y_lo), z: 4, core: 2. Of those that a mesh axis runs over, the one named last changes fastest.
Arguments:
- tokens: bfloat16 [2, 1024, 8192], P('dp', 'seq'), may hold values from -6 to 6
- in_weight: bfloat16 [8192, 3, 4096], P('seq', None, 'chan'), may hold values from -0.0625 to 0.0625
- short_taps: float32 [3, 3, 4096], P(None, None, 'chan'), may hold values from -1 to 1
- long_filter: float32 [1024, 4096], P('seq', 'chan'), may hold values from -1.25 to 1.25
- skip_gain: float32 [4096], P('chan'), may hold values from 0.5 to 1.5
- cotangent: bfloat16 [2, 1024, 4096], P('dp', 'seq', 'chan'), may hold values from -6 to 6
Outputs:
- hyena_out: bfloat16 [2, 1024, 4096], P('dp', 'seq', 'chan')
- grad_tokens: bfloat16 [2, 1024, 8192], P('dp', None, ('seq', 'chan'))
- grad_weight: bfloat16 [8192, 3, 4096], P('seq', None, 'chan')
- grad_filter: float32 [1024, 4096], P('seq', 'chan')
All inputs are finite; a program needn't handle non-finite values.
Results may differ from a plain program's by a relative error of at most 0.02.
Values may be sent and summed in bfloat16 or wider, within the bound.
No kernel may reach another device: no remote copies, remote signals or barrier semaphores. Data moves between devices by JAX's collectives and lax.ppermute only.
A program may use at most 128 MiB of HBM per device.

v0:
```python
import math
import jax
import jax.numpy as jnp
from jax import lax
from jax.sharding import PartitionSpec as P


def partner_2(shard, axis, stride):
    return lax.ppermute(shard, axis, [(i, i ^ 1 << stride) for i in range(lax.axis_size(axis))])


def shifted(value, axis, steps):
    count = lax.axis_size(axis)
    leading, last = (max(0, -steps), min(count, count - steps))
    return lax.ppermute(value, axis, [(source, source + steps) for source in range(leading, last)])


def complex_mul(left, right):
    return jnp.stack(
        [left[0] * right[0] - left[1] * right[1], left[0] * right[1] + left[1] * right[0]]
    )


def conjugate(signal):
    return jnp.stack([signal[0], -signal[1]])


def dft_tables(length):
    index = jnp.arange(length, dtype=jnp.int32)
    product = index[:, None] * index[None, :] % length
    phases = 2.0 * math.pi / length * product.astype(jnp.float32)
    return (jnp.cos(phases), jnp.sin(phases))


def table_apply(cos_table, sin_table, sign, signal, form):
    high = lax.Precision.HIGHEST
    real_cos = jnp.einsum(form, cos_table, signal[0], precision=high)
    imag_cos = jnp.einsum(form, cos_table, signal[1], precision=high)
    real_sin = jnp.einsum(form, sin_table, signal[0], precision=high)
    imag_sin = jnp.einsum(form, sin_table, signal[1], precision=high)
    return jnp.stack([real_cos - sign * imag_sin, imag_cos + sign * real_sin])


def reverse_bits(seq_pos, seq_count):
    bit_total = seq_count.bit_length() - 1
    result = jnp.zeros((), jnp.int32)
    for bit_pos in range(bit_total):
        result = result + seq_pos // (1 << bit_pos) % 2 * (1 << bit_total - 1 - bit_pos)
    return result


def pairs_forward(signal, seq_count, seq_pos):
    bit_total = seq_count.bit_length() - 1
    for bit_pos in reversed(range(bit_total)):
        half_span = 1 << bit_pos
        partner = partner_2(signal, "seq", bit_pos)
        offset = (seq_pos % half_span).astype(jnp.float32)
        phases = -math.pi * offset / half_span
        twiddle = jnp.stack([jnp.cos(phases), jnp.sin(phases)])
        is_upper = seq_pos // half_span % 2 == 1
        signal = jnp.where(is_upper, complex_mul(partner - signal, twiddle), signal + partner)
    return signal


def pairs_inverse(signal, seq_count, seq_pos):
    bit_total = seq_count.bit_length() - 1
    for bit_pos in range(bit_total):
        half_span = 1 << bit_pos
        partner = partner_2(signal.astype(jnp.bfloat16), "seq", bit_pos).astype(signal.dtype)
        offset = (seq_pos % half_span).astype(jnp.float32)
        phases = math.pi * offset / half_span
        twiddle = jnp.stack([jnp.cos(phases), jnp.sin(phases)])
        is_upper = seq_pos // half_span % 2 == 1
        signal = jnp.where(
            is_upper, partner - complex_mul(signal, twiddle), signal + complex_mul(partner, twiddle)
        )
    return signal


def position_twiddle(spec_order, tok_rows, full_len, sign):
    k_index = 2 * spec_order + jnp.arange(2, dtype=jnp.int32)
    pos_rows = jnp.arange(tok_rows, dtype=jnp.int32)
    product = k_index[:, None] * pos_rows[None, :] % full_len
    phases = sign * 2.0 * math.pi / full_len * product.astype(jnp.float32)
    return jnp.stack([jnp.cos(phases), jnp.sin(phases)])[:, None, :, :, None]


def forward_spectrum(rows_in, seq_count, seq_pos):
    tok_rows = rows_in.shape[1]
    full_len = 2 * seq_count * tok_rows
    phase_shift = math.pi * seq_pos.astype(jnp.float32) / seq_count
    real_part = jnp.stack([rows_in, rows_in * jnp.cos(phase_shift)], axis=1)
    imag_part = jnp.stack([jnp.zeros_like(rows_in), -rows_in * jnp.sin(phase_shift)], axis=1)
    signal = jnp.stack([real_part, imag_part])
    signal = pairs_forward(signal, seq_count, seq_pos)
    spec_order = reverse_bits(seq_pos, seq_count)
    signal = complex_mul(signal, position_twiddle(spec_order, tok_rows, full_len, -1.0))
    cos_table, sin_table = dft_tables(tok_rows)
    return table_apply(cos_table, sin_table, -1.0, signal, "ka,gbac->gbkc")


def inverse_spectrum(signal, seq_count, seq_pos):
    tok_rows = signal.shape[3]
    full_len = 2 * seq_count * tok_rows
    cos_table, sin_table = dft_tables(tok_rows)
    signal = table_apply(cos_table, sin_table, 1.0, signal, "ka,gbac->gbkc")
    spec_order = reverse_bits(seq_pos, seq_count)
    signal = complex_mul(signal, position_twiddle(spec_order, tok_rows, full_len, 1.0))
    signal = pairs_inverse(signal, seq_count, seq_pos)
    phase_shift = math.pi * seq_pos.astype(jnp.float32) / seq_count
    combined = (
        signal[0][:, 0]
        + jnp.cos(phase_shift) * signal[0][:, 1]
        - jnp.sin(phase_shift) * signal[1][:, 1]
    )
    return combined / full_len


def local(tokens, in_weight, short_taps, long_filter, skip_gain, cotangent):
    seq_count = lax.axis_size("seq")
    seq_pos = lax.axis_index("seq")
    tok_rows = tokens.shape[1]
    slab_rows = in_weight.shape[0]
    chan_cols = in_weight.shape[2]
    taps_len = short_taps.shape[1]
    grad_scale = 1.0 / math.sqrt(lax.axis_size("dp") * seq_count * tok_rows)
    spread = lax.all_to_all(tokens[0], "seq", split_axis=1, concat_axis=0, tiled=True)
    flat_weight = in_weight.reshape(slab_rows, 3 * chan_cols)
    projected = lax.psum_scatter(
        jnp.dot(spread, flat_weight, preferred_element_type=jnp.float32),
        "seq",
        scatter_dimension=0,
        tiled=True,
    ).reshape(tok_rows, 3, chan_cols)
    rim_rows = shifted(projected[tok_rows - (taps_len - 1) :], "seq", 1)
    extended = jnp.concatenate([rim_rows, projected], axis=0)
    streams = jnp.zeros_like(projected)
    for tap_pos in range(taps_len):
        begin = taps_len - 1 - tap_pos
        streams = streams + short_taps[:, tap_pos, :] * extended[begin : begin + tok_rows]
    queries = streams[:, 0]
    keys_in = streams[:, 1]
    values_in = streams[:, 2]
    gated_in = keys_in * values_in
    spectra = forward_spectrum(jnp.stack([gated_in, long_filter]), seq_count, seq_pos)
    gated_freq = spectra[:, 0:1]
    filter_freq = spectra[:, 1:2]
    conv_out = (
        inverse_spectrum(complex_mul(gated_freq, filter_freq), seq_count, seq_pos)[0]
        + skip_gain * gated_in
    )
    hyena_out = (queries * conv_out).astype(jnp.bfloat16)[None]
    grad_in = cotangent[0].astype(jnp.float32)
    d_conv = grad_in * queries
    d_query = grad_in * conv_out
    conv_freq = forward_spectrum(d_conv[None], seq_count, seq_pos)
    pair_freq = jnp.concatenate(
        [
            complex_mul(conjugate(filter_freq), conv_freq),
            complex_mul(conjugate(gated_freq), conv_freq),
        ],
        axis=1,
    )
    back_rows = inverse_spectrum(pair_freq, seq_count, seq_pos)
    d_gated = back_rows[0] + skip_gain * d_conv
    filter_part = back_rows[1] * grad_scale
    d_streams = jnp.stack([d_query, d_gated * values_in, d_gated * keys_in], axis=1)
    rim_next = shifted(d_streams[: taps_len - 1], "seq", -1)
    ext_next = jnp.concatenate([d_streams, rim_next], axis=0)
    d_projected = jnp.zeros_like(d_streams)
    for tap_pos in range(taps_len):
        d_projected = (
            d_projected + short_taps[:, tap_pos, :] * ext_next[tap_pos : tap_pos + tok_rows]
        )
    d_projected = d_projected.astype(jnp.bfloat16).reshape(tok_rows, 3 * chan_cols)
    shard_rows = lax.all_gather(d_projected, "seq", axis=0, tiled=True)
    weight_total = lax.dot_general(
        spread, shard_rows, (((0,), (0,)), ((), ())), preferred_element_type=jnp.float32
    )
    token_block = lax.dot_general(
        shard_rows, flat_weight, (((1,), (1,)), ((), ())), preferred_element_type=jnp.float32
    )
    grad_tokens = lax.psum_scatter(
        token_block.astype(jnp.bfloat16), "chan", scatter_dimension=1, tiled=True
    )[None]
    weight_sum, filter_sum = (
        lax.psum((weight_total * grad_scale).astype(jnp.bfloat16), "dp").astype(jnp.float32),
        lax.psum(filter_part.astype(jnp.bfloat16), "dp").astype(jnp.float32),
    )
    grad_weight = weight_sum.astype(jnp.bfloat16).reshape(slab_rows, 3, chan_cols)
    return (hyena_out, grad_tokens, grad_weight, filter_sum)


def solution(mesh):
    placed = (
        P("dp", "seq", None),
        P("seq", None, "chan"),
        P(None, None, "chan"),
        P("seq", "chan"),
        P("chan"),
        P("dp", "seq", "chan"),
    )
    return jax.shard_map(
        local,
        mesh=mesh,
        in_specs=placed,
        out_specs=(
            P("dp", "seq", "chan"),
            P("dp", None, ("seq", "chan")),
            P("seq", None, "chan"),
            P("seq", "chan"),
        ),
        check_vma=False,
    )
```

profile of v0, /device:TPU:0, one launch (start us, length us, event | category | flops | bytes accessed | tf_op | source)
XLA Modules:
  0.0 742.5 jit_solution(11029934226150978450)
XLA Ops:
  7.2 4.1 copy.90
  11.3 8.0 %all-to-all-start = ((bf16[128,8,1024]{0,2,1:T(8,128)(2,1)}), bf16[128,8,1024]{0,2,1:T(8,128)(2,1)S(1)}, u32[]{:S(2)}, u32[]{:S(2)}) async-start(bf16[128,8,1024]{0,2,1:T(8,128)(2,1)} %bitcast.318), calls=%async_computation | async-start | bytes 4194304 | tf_op jit(solution)/shard_map/all_to_all | solution.py:127
  19.3 4.6 copy.92
  24.0 23.8 %all-to-all-done = bf16[128,8,1024]{0,2,1:T(8,128)(2,1)S(1)} async-done(((bf16[128,8,1024]{0,2,1:T(8,128)(2,1)}), bf16[128,8,1024]{0,2,1:T(8,128)(2,1)S(1)}, u32[]{:S(2)}, u32[]{:S(2)}) %all-to-all-start) | async-done | bytes 2097184 | tf_op jit(solution)/shard_map/all_to_all | solution.py:127
  47.8 2.6 copy.91
  50.4 8.6 %fusion.204 = f32[1024,1536]{1,0:T(8,128)} fusion(bf16[1024,1024]{1,0:T(8,128)(2,1)} %bitcast.327, bf16[1024,1536]{0,1:T(8,128)(2,1)} %bitcast.323), kind=kOutput, calls=%fused_computation.316 | convolution fusion | flops 3221225472 | bytes 11534336 | tf_op jit(solution)/shard_map/dot_general | solution.py:130
  59.7 95.1 %reduce-scatter.5.cloned.1.call-done = f32[128,1536]{1,0:T(8,128)} async-done(((f32[1024,1536]{1,0:T(8,128)}), f32[128,1536]{1,0:T(8,128)}) %reduce-scatter.5.cloned.1.call-update) | async-done | bytes 786448 | tf_op jit(solution)/shard_map/reduce_scatter | solution.py:129
  155.7 2.4 collective-permute-start
  158.3 1.4 copy.93
  161.0 1.7 pad_maximum_fusion
  162.6 4.8 collective-permute-start.1
  167.7 44.0 %collective-permute-done.1 = f32[2,2,2,128,512]{4,3,1,2,0:T(8,128)} collective-permute-done((f32[2,2,2,128,512]{4,3,1,2,0:T(8,128)}, f32[2,2,2,128,512]{4,3,1,2,0:T(8,128)}, u32[]{:S(2)}, u32[]{:S(2)}) %collective-permute-start.1) | collective-permute-done | bytes 2097184 | tf_op jit(solution)/shard_map/ppermute | solution.py:9
  211.6 2.1 fusion.183
  214.0 4.5 maximum_select_fusion
  218.5 2.0 collective-permute-start.2
  220.7 43.1 %collective-permute-done.2 = f32[2,2,2,128,512]{4,3,1,2,0:T(8,128)} collective-permute-done((f32[2,2,2,128,512]{4,3,1,2,0:T(8,128)}, f32[2,2,2,128,512]{4,3,1,2,0:T(8,128)}, u32[]{:S(2)}, u32[]{:S(2)}) %collective-permute-start.2) | collective-permute-done | bytes 2097184 | tf_op jit(solution)/shard_map/ppermute | solution.py:9
  263.8 3.8 fusion.212
  269.1 4.9 maximum_select_fusion.1
  274.0 2.2 collective-permute-start.3
  276.4 43.6 %collective-permute-done.3 = f32[2,2,2,128,512]{4,3,1,2,0:T(8,128)S(1)} collective-permute-done((f32[2,2,2,128,512]{4,3,1,2,0:T(8,128)}, f32[2,2,2,128,512]{4,3,1,2,0:T(8,128)S(1)}, u32[]{:S(2)}, u32[]{:S(2)}) %collective-permute-start.3) | collective-permute-done | bytes 2097184 | tf_op jit(solution)/shard_map/ppermute | solution.py:9
  319.9 2.1 sub.247
  322.2 2.4 maximum_select_fusion.2
  324.9 1.9 fusion.30
  326.9 1.9 fusion.26
  328.8 2.0 fusion.7
  330.8 2.0 fusion.5
  334.7 1.1 fusion.12
  337.0 2.2 collective-permute-start.4
  339.2 8.7 %collective-permute-done.4 = bf16[2,1,2,128,512]{4,3,2,1,0:T(8,128)(2,1)S(1)} collective-permute-done((bf16[2,1,2,128,512]{4,3,2,1,0:T(8,128)(2,1)S(1)}, bf16[2,1,2,128,512]{4,3,2,1,0:T(8,128)(2,1)S(1)}, u32[]{:S(2)}, u32[]{:S(2)}) %collective-permute-start.4) | collective-permute-done | bytes 524320 | tf_op jit(solution)/shard_map/ppermute | solution.py:9
  348.7 1.8 collective-permute-start.5
  350.7 8.8 %collective-permute-done.5 = bf16[2,1,2,128,512]{4,3,2,1,0:T(8,128)(2,1)S(1)} collective-permute-done((bf16[2,1,2,128,512]{4,3,2,1,0:T(8,128)(2,1)S(1)}, bf16[2,1,2,128,512]{4,3,2,1,0:T(8,128)(2,1)S(1)}, u32[]{:S(2)}, u32[]{:S(2)}) %collective-permute-start.5) | collective-permute-done | bytes 524320 | tf_op jit(solution)/shard_map/ppermute | solution.py:9
  359.8 1.2 fusion.189
  362.4 10.9 %collective-permute-done.6 = bf16[2,1,2,128,512]{4,3,2,1,0:T(8,128)(2,1)S(1)} collective-permute-done((bf16[2,1,2,128,512]{4,3,2,1,0:T(8,128)(2,1)}, bf16[2,1,2,128,512]{4,3,2,1,0:T(8,128)(2,1)S(1)}, u32[]{:S(2)}, u32[]{:S(2)}) %collective-permute-start.6) | collective-permute-done | bytes 524320 | tf_op jit(solution)/shard_map/ppermute | solution.py:9
  375.9 23.1 %collective-permute-done.7 = f32[2,1,2,128,512]{4,3,2,1,0:T(8,128)S(1)} collective-permute-done((f32[2,1,2,128,512]{4,3,2,1,0:T(8,128)S(1)}, f32[2,1,2,128,512]{4,3,2,1,0:T(8,128)S(1)}, u32[]{:S(2)}, u32[]{:S(2)}) %collective-permute-start.7) | collective-permute-done | bytes 1048608 | tf_op jit(solution)/shard_map/ppermute | solution.py:9
  399.7 2.9 collective-permute-start.8
  402.6 12.8 %collective-permute-done.8 = f32[2,1,2,128,512]{4,3,2,1,0:T(8,128)S(1)} collective-permute-done((f32[2,1,2,128,512]{4,3,2,1,0:T(8,128)S(1)}, f32[2,1,2,128,512]{4,3,2,1,0:T(8,128)S(1)}, u32[]{:S(2)}, u32[]{:S(2)}) %collective-permute-start.8) | collective-permute-done | bytes 1048608 | tf_op jit(solution)/shard_map/ppermute | solution.py:9
  416.7 4.4 collective-permute-start.9
  421.1 12.8 %collective-permute-done.9 = f32[2,1,2,128,512]{4,3,2,1,0:T(8,128)S(1)} collective-permute-done((f32[2,1,2,128,512]{4,3,2,1,0:T(8,128)S(1)}, f32[2,1,2,128,512]{4,3,2,1,0:T(8,128)S(1)}, u32[]{:S(2)}, u32[]{:S(2)}) %collective-permute-start.9) | collective-permute-done | bytes 1048608 | tf_op jit(solution)/shard_map/ppermute | solution.py:9
  435.0 1.2 fusion.75
  436.2 1.2 fusion.74
  437.4 1.2 fusion.11
  438.6 1.3 fusion.49
  440.2 1.3 fusion.20
  441.5 1.3 fusion.24
  442.8 1.3 convolution_add_fusion
  444.2 1.6 fusion.19
  446.0 3.8 collective-permute-start.10
  450.0 12.6 %collective-permute-done.10 = bf16[2,2,2,128,512]{4,3,1,2,0:T(8,128)(2,1)S(1)} collective-permute-done((bf16[2,2,2,128,512]{4,3,1,2,0:T(8,128)(2,1)S(1)}, bf16[2,2,2,128,512]{4,3,1,2,0:T(8,128)(2,1)S(1)}, u32[]{:S(2)}, u32[]{:S(2)}) %collective-permute-start.10) | collective-permute-done | bytes 1048608 | tf_op jit(solution)/shard_map/ppermute | solution.py:9
  464.1 2.1 collective-permute-start.11
  466.6 12.4 %collective-permute-done.11 = bf16[2,2,2,128,512]{4,3,1,2,0:T(8,128)(2,1)S(1)} collective-permute-done((bf16[2,2,2,128,512]{4,3,1,2,0:T(8,128)(2,1)S(1)}, bf16[2,2,2,128,512]{4,3,1,2,0:T(8,128)(2,1)S(1)}, u32[]{:S(2)}, u32[]{:S(2)}) %collective-permute-start.11) | collective-permute-done | bytes 1048608 | tf_op jit(solution)/shard_map/ppermute | solution.py:9
  480.5 17.3 %collective-permute-start.12 = (bf16[2,2,2,128,512]{4,3,1,2,0:T(8,128)(2,1)S(1)}, bf16[2,2,2,128,512]{4,3,1,2,0:T(8,128)(2,1)S(1)}, u32[]{:S(2)}, u32[]{:S(2)}) collective-permute-start(bf16[2,2,2,128,512]{4,3,1,2,0:T(8,128)(2,1)S(1)} %get-tuple-element.8), channel_id=1, source_target_pairs={{0,64},{16,80},{32,96},{48,112},{64,0},{80,16},{96,32},{112,48},{1... | collective-permute-start | bytes 3145736 | tf_op jit(solution)/shard_map/ppermute | solution.py:9
  498.2 12.5 %collective-permute-done.12 = bf16[2,2,2,128,512]{4,3,1,2,0:T(8,128)(2,1)S(1)} collective-permute-done((bf16[2,2,2,128,512]{4,3,1,2,0:T(8,128)(2,1)S(1)}, bf16[2,2,2,128,512]{4,3,1,2,0:T(8,128)(2,1)S(1)}, u32[]{:S(2)}, u32[]{:S(2)}) %collective-permute-start.12) | collective-permute-done | bytes 1048608 | tf_op jit(solution)/shard_map/ppermute | solution.py:9
  512.8 1.3 collective-permute-start.13
  514.1 5.8 collective-permute-done.13
  521.9 65.9 %all-gather.2.cloned.1.call-done = bf16[1024,1536]{0,1:T(8,128)(2,1)} async-done(((bf16[128,1536]{0,1:T(8,128)(2,1)}), bf16[1024,1536]{0,1:T(8,128)(2,1)}) %all-gather.2.cloned.1.call-update) | async-done | bytes 3145744 | tf_op jit(solution)/shard_map/all_gather | solution.py:176
  587.8 6.8 multiply_convert_fusion
  594.6 4.7 copy.118
  599.6 6.3 convolution_convert_fusion
  605.9 2.6 copy.149
  608.5 84.1 %all-reduce.5.cloned.1.call-done = (bf16[1024,3,512]{2,0,1:T(8,128)(2,1)}, bf16[128,512]{1,0:T(8,128)(2,1)}) async-done(((bf16[1024,3,512]{2,0,1:T(8,128)(2,1)}, bf16[128,512]{1,0:T(8,128)(2,1)}), (bf16[1024,3,512]{2,0,1:T(8,128)(2,1)}, bf16[128,512]{1,0:T(8,128)(2,1)})) %all-reduce.5.cloned.1.call-update) | async-done | bytes 3276816 | tf_op jit(solution)/shard_map/psum | solution.py:187
  692.6 1.6 convert_element_type.209
  694.3 35.9 %reduce-scatter.7.cloned.1.call-done = bf16[128,1024]{1,0:T(8,128)(2,1)} async-done(((bf16[1024,1024]{1,0:T(8,128)(2,1)}), bf16[128,1024]{1,0:T(8,128)(2,1)}) %reduce-scatter.7.cloned.1.call-update) | async-done | bytes 262160
  730.2 1.8 copy.150
  731.9 3.8 copy.178
  (131 shorter events, 25.1 us)
Async XLA Ops:
  11.3 36.5 %all-to-all-start = ((bf16[128,8,1024]{0,2,1:T(8,128)(2,1)}), bf16[128,8,1024]{0,2,1:T(8,128)(2,1)S(1)}, u32[]{:S(2)}, u32[]{:S(2)}) async-start(bf16[128,8,1024]{0,2,1:T(8,128)(2,1)} %bitcast.318), calls=%async_computation | async-start | bytes 4194304 | tf_op jit(solution)/shard_map/all_to_all | solution.py:127
  19.3 135.6 %reduce-scatter.5.cloned.1.call-start = ((), (), s32[]{:S(2)}) async-start(), calls=%async_computation.3 | async-start | bytes 7077888 | tf_op jit(solution)/shard_map/reduce_scatter | solution.py:129
  59.0 0.7 copy-start.18
  59.0 528.8 %all-gather.2.cloned.1.call-start = ((), (), s32[]{:S(2)}) async-start(), calls=%async_computation.4 | async-start | bytes 3538944 | tf_op jit(solution)/shard_map/all_gather | solution.py:176
  155.7 4.3 collective-permute-start
  158.3 2.0 copy-start.11
  159.7 1.0 copy-start.10
  162.6 49.0 %collective-permute-start.1 = (f32[2,2,2,128,512]{4,3,1,2,0:T(8,128)}, f32[2,2,2,128,512]{4,3,1,2,0:T(8,128)}, u32[]{:S(2)}, u32[]{:S(2)}) collective-permute-start(f32[2,2,2,128,512]{4,3,1,2,0:T(8,128)} %pad_maximum_fusion), channel_id=1, source_target_pairs={{0,64},{16,80},{32,96},{48,112},{64,0},{80,16},{96,32},{112,48},{1... | collective-permute-start | bytes 6291464 | tf_op jit(solution)/shard_map/ppermute | solution.py:9
  214.0 4.5 copy-start
  214.0 4.5 copy-start.2
  218.5 45.3 %collective-permute-start.2 = (f32[2,2,2,128,512]{4,3,1,2,0:T(8,128)}, f32[2,2,2,128,512]{4,3,1,2,0:T(8,128)}, u32[]{:S(2)}, u32[]{:S(2)}) collective-permute-start(f32[2,2,2,128,512]{4,3,1,2,0:T(8,128)} %maximum_select_fusion), channel_id=1, source_target_pairs={{0,32},{16,48},{32,0},{48,16},{64,96},{80,112},{96,64},{112,80},{1... | collective-permute-start | bytes 6291464 | tf_op jit(solution)/shard_map/ppermute | solution.py:9
  267.6 1.2 copy-start.1
  267.6 1.5 copy-start.3
  274.0 45.9 %collective-permute-start.3 = (f32[2,2,2,128,512]{4,3,1,2,0:T(8,128)}, f32[2,2,2,128,512]{4,3,1,2,0:T(8,128)S(1)}, u32[]{:S(2)}, u32[]{:S(2)}) collective-permute-start(f32[2,2,2,128,512]{4,3,1,2,0:T(8,128)} %maximum_select_fusion.1), channel_id=1, source_target_pairs={{0,16},{16,0},{32,48},{48,32},{64,80},{80,64},{96,112},{112,96},{1... | collective-permute-start | bytes 6291464 | tf_op jit(solution)/shard_map/ppermute | solution.py:9
  276.3 48.3 %copy-start.13 = (f32[2,128]{1,0:T(2,128)}, f32[2,128]{1,0:T(2,128)S(1)}, u32[]{:S(2)}) copy-start(f32[2,128]{1,0:T(2,128)S(1)} %get-tuple-element.80) | copy-start | bytes 3076
  276.3 48.3 %copy-start.15 = (f32[2,128]{1,0:T(2,128)}, f32[2,128]{1,0:T(2,128)S(1)}, u32[]{:S(2)}) copy-start(f32[2,128]{1,0:T(2,128)S(1)} %get-tuple-element.81) | copy-start | bytes 3076
  276.3 59.5 %copy-start.19 = (f32[2,128]{1,0:T(2,128)}, f32[2,128]{1,0:T(2,128)S(1)}, u32[]{:S(2)}) copy-start(f32[2,128]{1,0:T(2,128)S(1)} %get-tuple-element.78) | copy-start | bytes 3076
  276.3 59.5 %copy-start.21 = (f32[2,128]{1,0:T(2,128)}, f32[2,128]{1,0:T(2,128)S(1)}, u32[]{:S(2)}) copy-start(f32[2,128]{1,0:T(2,128)S(1)} %get-tuple-element.79) | copy-start | bytes 3076
  330.8 2.1 copy-start.4
  332.8 1.0 copy-start.6
  337.0 11.0 %collective-permute-start.4 = (bf16[2,1,2,128,512]{4,3,2,1,0:T(8,128)(2,1)S(1)}, bf16[2,1,2,128,512]{4,3,2,1,0:T(8,128)(2,1)S(1)}, u32[]{:S(2)}, u32[]{:S(2)}) collective-permute-start(bf16[2,1,2,128,512]{4,3,2,1,0:T(8,128)(2,1)S(1)} %fusion.32), channel_id=1, source_target_pairs={{0,16},{16,0},{32,48},{48,32},{64,80},{80,64},{96,112},{112,96},{1... | collective-permute-start | bytes 1572872 | tf_op jit(solution)/shard_map/ppermute | solution.py:9
  348.7 10.9 %collective-permute-start.5 = (bf16[2,1,2,128,512]{4,3,2,1,0:T(8,128)(2,1)S(1)}, bf16[2,1,2,128,512]{4,3,2,1,0:T(8,128)(2,1)S(1)}, u32[]{:S(2)}, u32[]{:S(2)}) collective-permute-start(bf16[2,1,2,128,512]{4,3,2,1,0:T(8,128)(2,1)S(1)} %get-tuple-element.17), channel_id=1, source_target_pairs={{0,32},{16,48},{32,0},{48,16},{64,96},{80,112},{96,64},{112,80},{1... | collective-permute-start | bytes 1572872 | tf_op jit(solution)/shard_map/ppermute | solution.py:9
  359.8 2.4 copy-start.9
  361.0 12.3 %collective-permute-start.6 = (bf16[2,1,2,128,512]{4,3,2,1,0:T(8,128)(2,1)}, bf16[2,1,2,128,512]{4,3,2,1,0:T(8,128)(2,1)S(1)}, u32[]{:S(2)}, u32[]{:S(2)}) collective-permute-start(bf16[2,1,2,128,512]{4,3,2,1,0:T(8,128)(2,1)} %get-tuple-element.15), channel_id=1, source_target_pairs={{0,64},{16,80},{32,96},{48,112},{64,0},{80,16},{96,32},{112,48},{1... | collective-permute-start | bytes 1572872 | tf_op jit(solution)/shard_map/ppermute | solution.py:9
  374.0 0.7 copy-start.17
  375.8 23.2 %collective-permute-start.7 = (f32[2,1,2,128,512]{4,3,2,1,0:T(8,128)S(1)}, f32[2,1,2,128,512]{4,3,2,1,0:T(8,128)S(1)}, u32[]{:S(2)}, u32[]{:S(2)}) collective-permute-start(f32[2,1,2,128,512]{4,3,2,1,0:T(8,128)S(1)} %pad_maximum_fusion.3), channel_id=1, source_target_pairs={{0,64},{16,80},{32,96},{48,112},{64,0},{80,16},{96,32},{112,48},{1... | collective-permute-start | bytes 3145736 | tf_op jit(solution)/shard_map/ppermute | solution.py:9
  399.7 15.6 %collective-permute-start.8 = (f32[2,1,2,128,512]{4,3,2,1,0:T(8,128)S(1)}, f32[2,1,2,128,512]{4,3,2,1,0:T(8,128)S(1)}, u32[]{:S(2)}, u32[]{:S(2)}) collective-permute-start(f32[2,1,2,128,512]{4,3,2,1,0:T(8,128)S(1)} %maximum_select_fusion.3), channel_id=1, source_target_pairs={{0,32},{16,48},{32,0},{48,16},{64,96},{80,112},{96,64},{112,80},{1... | collective-permute-start | bytes 3145736 | tf_op jit(solution)/shard_map/ppermute | solution.py:9
  416.7 17.2 %collective-permute-start.9 = (f32[2,1,2,128,512]{4,3,2,1,0:T(8,128)S(1)}, f32[2,1,2,128,512]{4,3,2,1,0:T(8,128)S(1)}, u32[]{:S(2)}, u32[]{:S(2)}) collective-permute-start(f32[2,1,2,128,512]{4,3,2,1,0:T(8,128)S(1)} %maximum_select_fusion.4), channel_id=1, source_target_pairs={{0,16},{16,0},{32,48},{48,32},{64,80},{80,64},{96,112},{112,96},{1... | collective-permute-start | bytes 3145736 | tf_op jit(solution)/shard_map/ppermute | solution.py:9
  434.3 0.7 copy-start.14
  434.3 0.7 copy-start.16
  435.0 3.6 copy-start.5
  435.0 3.6 copy-start.7
  442.8 1.3 copy-start.20
  442.8 1.3 copy-start.22
  446.0 16.6 %collective-permute-start.10 = (bf16[2,2,2,128,512]{4,3,1,2,0:T(8,128)(2,1)S(1)}, bf16[2,2,2,128,512]{4,3,1,2,0:T(8,128)(2,1)S(1)}, u32[]{:S(2)}, u32[]{:S(2)}) collective-permute-start(bf16[2,2,2,128,512]{4,3,1,2,0:T(8,128)(2,1)S(1)} %fusion.3), channel_id=1, source_target_pairs={{0,16},{16,0},{32,48},{48,32},{64,80},{80,64},{96,112},{112,96},{1... | collective-permute-start | bytes 3145736 | tf_op jit(solution)/shard_map/ppermute | solution.py:9
  464.1 14.9 %collective-permute-start.11 = (bf16[2,2,2,128,512]{4,3,1,2,0:T(8,128)(2,1)S(1)}, bf16[2,2,2,128,512]{4,3,1,2,0:T(8,128)(2,1)S(1)}, u32[]{:S(2)}, u32[]{:S(2)}) collective-permute-start(bf16[2,2,2,128,512]{4,3,1,2,0:T(8,128)(2,1)S(1)} %get-tuple-element.10), channel_id=1, source_target_pairs={{0,32},{16,48},{32,0},{48,16},{64,96},{80,112},{96,64},{112,80},{1... | collective-permute-start | bytes 3145736 | tf_op jit(solution)/shard_map/ppermute | solution.py:9
  480.5 30.1 %collective-permute-start.12 = (bf16[2,2,2,128,512]{4,3,1,2,0:T(8,128)(2,1)S(1)}, bf16[2,2,2,128,512]{4,3,1,2,0:T(8,128)(2,1)S(1)}, u32[]{:S(2)}, u32[]{:S(2)}) collective-permute-start(bf16[2,2,2,128,512]{4,3,1,2,0:T(8,128)(2,1)S(1)} %get-tuple-element.8), channel_id=1, source_target_pairs={{0,64},{16,80},{32,96},{48,112},{64,0},{80,16},{96,32},{112,48},{1... | collective-permute-start | bytes 3145736 | tf_op jit(solution)/shard_map/ppermute | solution.py:9
  512.6 7.4 copy-start.12
  512.8 7.1 collective-permute-start.13
  519.9 67.8 %copy-start.8 = (bf16[8,128,1024]{2,1,0:T(8,128)(2,1)S(1)}, bf16[8,128,1024]{2,1,0:T(8,128)(2,1)}, u32[]{:S(2)}) copy-start(bf16[8,128,1024]{2,1,0:T(8,128)(2,1)} %copy.91) | copy-start | bytes 6291460
  521.2 171.4 %all-reduce.5.cloned.1.call-start = ((), (), s32[]{:S(2)}) async-start(), calls=%async_computation.6 | async-start | bytes 6553600 | tf_op jit(solution)/shard_map/psum | solution.py:187
  599.3 130.9 %reduce-scatter.7.cloned.1.call-start = ((), (), s32[]{:S(2)}) async-start(), calls=%async_computation.5 | async-start | bytes 2359296
Sparse Core Ops, SparseCore 0:
  59.1 95.7 reduce-scatter.4
  521.3 66.4 all-gather.1
  599.4 93.1 all-reduce.4
  695.6 34.5 reduce-scatter.6
where the time goes:
time: 751 us; the launch traced here: 742 us
  waiting for transfers between devices  556 us (74%)
  starting transfers between devices  56.6 us (8%)
  matrix products  43.9 us (6%)
  other arithmetic  39.1 us (5%)
  local copies, waits for them, and re-layouts  31.3 us (4%)
  between operations  15.8 us (2%)
    ppermute x12, waiting for transfers between devices, partner_2(): lax.ppermute(shard, axis, [(i, i ^ 1 << stride) for i in range(lax.axis_s...  245 us
    reduce_scatter x1, waiting for transfers between devices, local(): lax.psum_scatter(jnp.dot(spread, flat_weight, preferred_element_type=jnp....  95.1 us
    psum x1, waiting for transfers between devices, local(): lax.psum((weight_total * grad_scale).astype(jnp.bfloat16), 'dp')  84.1 us
    all_gather x1, waiting for transfers between devices, local(): shard_rows = lax.all_gather(d_projected, 'seq', axis=0, tiled=True)  65.9 us
    ppermute x12, starting transfers between devices, partner_2(): lax.ppermute(shard, axis, [(i, i ^ 1 << stride) for i in range(lax.axis_s...  44.5 us
    unnamed x5, waiting for transfers between devices  36 us
    all_to_all x1, waiting for transfers between devices, local(): lax.all_to_all(tokens[0], 'seq', split_axis=1, concat_axis=0, tiled=True)  23.8 us
    unnamed x53, local copies, waits for them, and re-layouts  20 us
  transfers between devices with their start and end apart: 19, of which 18 were waited for; matrix products, arithmetic and copies ran while one was open for 3% of the time, Pallas kernels for 0%

commit v1 on v0

--- a/solution.py
+++ b/solution.py
@@ -184,7 +184,9 @@
         token_block.astype(jnp.bfloat16), "chan", scatter_dimension=1, tiled=True
     )[None]
     weight_sum, filter_sum = (
-        lax.psum((weight_total * grad_scale).astype(jnp.bfloat16), "dp").astype(jnp.float32),
+        jnp.sum(
+            lax.all_gather((weight_total * grad_scale).astype(jnp.bfloat16), "dp"), axis=0
+        ).astype(jnp.float32),
         lax.psum(filter_part.astype(jnp.bfloat16), "dp").astype(jnp.float32),
     )
     grad_weight = weight_sum.astype(jnp.bfloat16).reshape(slab_rows, 3, chan_cols)

time: 751 us -> 788 us (1.049)
  other arithmetic: 39.1 us -> 57.2 us
  waiting for transfers between devices: 556 us -> 565 us
  local copies, waits for them, and re-layouts: 31.3 us -> 39.9 us
    all_gather x0 -> x1, waiting for transfers between devices: none -> 82.1 us  [local(): lax.all_gather((weight_total * grad_scale).astype(jnp.bfloat16), 'dp')]
    psum x1, waiting for transfers between devices: 84.1 us -> 11.6 us  [local(): lax.psum(filter_part.astype(jnp.bfloat16), 'dp').astype(jnp.float32)]
    reduce_sum x0 -> x1, other arithmetic: none -> 18.2 us  [local(): jnp.sum(lax.all_gather((weight_total * grad_scale).astype(jnp.bfloat16),...]
    all_gather x0 -> x1, local copies, waits for them, and re-layouts: none -> 11.1 us  [local(): lax.all_gather((weight_total * grad_scale).astype(jnp.bfloat16), 'dp')]
    unnamed x5 -> x6, waiting for transfers between devices: 36 us -> 35.3 us
  transfers between devices with their start and end apart: 19 -> 20, of which waited for: 18 -> 19; matrix products, arithmetic and copies ran while one was open for 3% -> 4% of each run, Pallas kernels for 0% -> 0%
where the time goes in v1:
time: 788 us; the launch traced here: 778 us
  waiting for transfers between devices  565 us (72%)
  other arithmetic  57.2 us (7%)
  starting transfers between devices  56.6 us (7%)
  matrix products  43.9 us (6%)
  local copies, waits for them, and re-layouts  39.9 us (5%)
  between operations  16 us (2%)
    ppermute x12, waiting for transfers between devices, partner_2(): lax.ppermute(shard, axis, [(i, i ^ 1 << stride) for i in range(lax.axis_s...  245 us
    reduce_scatter x1, waiting for transfers between devices, local(): lax.psum_scatter(jnp.dot(spread, flat_weight, preferred_element_type=jnp....  95.4 us
    all_gather x1, waiting for transfers between devices, local(): lax.all_gather((weight_total * grad_scale).astype(jnp.bfloat16), 'dp')  82.1 us
    all_gather x1, waiting for transfers between devices, local(): shard_rows = lax.all_gather(d_projected, 'seq', axis=0, tiled=True)  66.1 us
    ppermute x12, starting transfers between devices, partner_2(): lax.ppermute(shard, axis, [(i, i ^ 1 << stride) for i in range(lax.axis_s...  44.4 us
    unnamed x6, waiting for transfers between devices  35.3 us
    all_to_all x1, waiting for transfers between devices, local(): lax.all_to_all(tokens[0], 'seq', split_axis=1, concat_axis=0, tiled=True)  23.8 us
    unnamed x53, local copies, waits for them, and re-layouts  22.2 us
  transfers between devices with their start and end apart: 20, of which 19 were waited for; matrix products, arithmetic and copies ran while one was open for 4% of the time, Pallas kernels for 0%

profile of v1, /device:TPU:0, one launch (start us, length us, event | category | flops | bytes accessed | tf_op | source)
XLA Modules:
  0.0 778.4 jit_solution(3475664948657681862)
XLA Ops:
  7.2 4.1 copy.89
  11.2 8.0 %all-to-all-start = ((bf16[128,8,1024]{0,2,1:T(8,128)(2,1)}), bf16[128,8,1024]{0,2,1:T(8,128)(2,1)S(1)}, u32[]{:S(2)}, u32[]{:S(2)}) async-start(bf16[128,8,1024]{0,2,1:T(8,128)(2,1)} %bitcast.321), calls=%async_computation | async-start | bytes 4194304 | tf_op jit(solution)/shard_map/all_to_all | solution.py:127
  19.3 4.6 copy.91
  24.0 23.8 %all-to-all-done = bf16[128,8,1024]{0,2,1:T(8,128)(2,1)S(1)} async-done(((bf16[128,8,1024]{0,2,1:T(8,128)(2,1)}), bf16[128,8,1024]{0,2,1:T(8,128)(2,1)S(1)}, u32[]{:S(2)}, u32[]{:S(2)}) %all-to-all-start) | async-done | bytes 2097184 | tf_op jit(solution)/shard_map/all_to_all | solution.py:127
  47.8 2.6 copy.90
  50.4 8.6 %fusion.205 = f32[1024,1536]{1,0:T(8,128)} fusion(bf16[1024,1024]{1,0:T(8,128)(2,1)} %bitcast.329, bf16[1024,1536]{0,1:T(8,128)(2,1)} %bitcast.326), kind=kOutput, calls=%fused_computation.317 | convolution fusion | flops 3221225472 | bytes 11534336 | tf_op jit(solution)/shard_map/dot_general | solution.py:130
  59.7 95.4 %reduce-scatter.5.cloned.1.call-done = f32[128,1536]{1,0:T(8,128)} async-done(((f32[1024,1536]{1,0:T(8,128)}), f32[128,1536]{1,0:T(8,128)}) %reduce-scatter.5.cloned.1.call-update) | async-done | bytes 786448 | tf_op jit(solution)/shard_map/reduce_scatter | solution.py:129
  155.9 2.4 collective-permute-start
  158.6 1.4 copy.92
  161.3 1.6 pad_maximum_fusion
  162.9 4.8 collective-permute-start.1
  167.9 44.0 %collective-permute-done.1 = f32[2,2,2,128,512]{4,3,1,2,0:T(8,128)} collective-permute-done((f32[2,2,2,128,512]{4,3,1,2,0:T(8,128)}, f32[2,2,2,128,512]{4,3,1,2,0:T(8,128)}, u32[]{:S(2)}, u32[]{:S(2)}) %collective-permute-start.1) | collective-permute-done | bytes 2097184 | tf_op jit(solution)/shard_map/ppermute | solution.py:9
  211.9 2.1 fusion.184
  214.3 4.5 maximum_select_fusion
  218.8 1.9 collective-permute-start.2
  220.9 43.2 %collective-permute-done.2 = f32[2,2,2,128,512]{4,3,1,2,0:T(8,128)} collective-permute-done((f32[2,2,2,128,512]{4,3,1,2,0:T(8,128)}, f32[2,2,2,128,512]{4,3,1,2,0:T(8,128)}, u32[]{:S(2)}, u32[]{:S(2)}) %collective-permute-start.2) | collective-permute-done | bytes 2097184 | tf_op jit(solution)/shard_map/ppermute | solution.py:9
  264.1 3.8 fusion.213
  269.4 4.9 maximum_select_fusion.1
  274.3 2.2 collective-permute-start.3
  276.7 43.6 %collective-permute-done.3 = f32[2,2,2,128,512]{4,3,1,2,0:T(8,128)S(1)} collective-permute-done((f32[2,2,2,128,512]{4,3,1,2,0:T(8,128)}, f32[2,2,2,128,512]{4,3,1,2,0:T(8,128)S(1)}, u32[]{:S(2)}, u32[]{:S(2)}) %collective-permute-start.3) | collective-permute-done | bytes 2097184 | tf_op jit(solution)/shard_map/ppermute | solution.py:9
  320.2 2.1 sub.247
  322.6 2.4 maximum_select_fusion.2
  325.3 1.9 fusion.27
  327.2 1.9 fusion.31
  329.2 2.0 fusion.6
  331.1 2.0 fusion.8
  335.0 1.3 fusion.13
  337.5 2.2 collective-permute-start.4
  339.8 8.7 %collective-permute-done.4 = bf16[2,1,2,128,512]{4,3,2,1,0:T(8,128)(2,1)S(1)} collective-permute-done((bf16[2,1,2,128,512]{4,3,2,1,0:T(8,128)(2,1)S(1)}, bf16[2,1,2,128,512]{4,3,2,1,0:T(8,128)(2,1)S(1)}, u32[]{:S(2)}, u32[]{:S(2)}) %collective-permute-start.4) | collective-permute-done | bytes 524320 | tf_op jit(solution)/shard_map/ppermute | solution.py:9
  349.2 1.8 collective-permute-start.5
  351.3 8.7 %collective-permute-done.5 = bf16[2,1,2,128,512]{4,3,2,1,0:T(8,128)(2,1)S(1)} collective-permute-done((bf16[2,1,2,128,512]{4,3,2,1,0:T(8,128)(2,1)S(1)}, bf16[2,1,2,128,512]{4,3,2,1,0:T(8,128)(2,1)S(1)}, u32[]{:S(2)}, u32[]{:S(2)}) %collective-permute-start.5) | collective-permute-done | bytes 524320 | tf_op jit(solution)/shard_map/ppermute | solution.py:9
  360.2 1.2 fusion.190
  362.9 10.8 %collective-permute-done.6 = bf16[2,1,2,128,512]{4,3,2,1,0:T(8,128)(2,1)S(1)} collective-permute-done((bf16[2,1,2,128,512]{4,3,2,1,0:T(8,128)(2,1)}, bf16[2,1,2,128,512]{4,3,2,1,0:T(8,128)(2,1)S(1)}, u32[]{:S(2)}, u32[]{:S(2)}) %collective-permute-start.6) | collective-permute-done | bytes 524320 | tf_op jit(solution)/shard_map/ppermute | solution.py:9
  376.3 22.9 %collective-permute-done.7 = f32[2,1,2,128,512]{4,3,2,1,0:T(8,128)S(1)} collective-permute-done((f32[2,1,2,128,512]{4,3,2,1,0:T(8,128)S(1)}, f32[2,1,2,128,512]{4,3,2,1,0:T(8,128)S(1)}, u32[]{:S(2)}, u32[]{:S(2)}) %collective-permute-start.7) | collective-permute-done | bytes 1048608 | tf_op jit(solution)/shard_map/ppermute | solution.py:9
  400.0 3.0 collective-permute-start.8
  403.0 12.8 %collective-permute-done.8 = f32[2,1,2,128,512]{4,3,2,1,0:T(8,128)S(1)} collective-permute-done((f32[2,1,2,128,512]{4,3,2,1,0:T(8,128)S(1)}, f32[2,1,2,128,512]{4,3,2,1,0:T(8,128)S(1)}, u32[]{:S(2)}, u32[]{:S(2)}) %collective-permute-start.8) | collective-permute-done | bytes 1048608 | tf_op jit(solution)/shard_map/ppermute | solution.py:9
  417.2 4.2 collective-permute-start.9
  421.3 12.8 %collective-permute-done.9 = f32[2,1,2,128,512]{4,3,2,1,0:T(8,128)S(1)} collective-permute-done((f32[2,1,2,128,512]{4,3,2,1,0:T(8,128)S(1)}, f32[2,1,2,128,512]{4,3,2,1,0:T(8,128)S(1)}, u32[]{:S(2)}, u32[]{:S(2)}) %collective-permute-start.9) | collective-permute-done | bytes 1048608 | tf_op jit(solution)/shard_map/ppermute | solution.py:9
  438.8 1.3 fusion.50
  440.4 1.3 fusion.21
  441.7 1.3 fusion.25
  443.0 1.3 convolution_add_fusion
  444.4 1.6 fusion.20
  446.1 3.8 collective-permute-start.10
  450.2 12.6 %collective-permute-done.10 = bf16[2,2,2,128,512]{4,3,1,2,0:T(8,128)(2,1)S(1)} collective-permute-done((bf16[2,2,2,128,512]{4,3,1,2,0:T(8,128)(2,1)S(1)}, bf16[2,2,2,128,512]{4,3,1,2,0:T(8,128)(2,1)S(1)}, u32[]{:S(2)}, u32[]{:S(2)}) %collective-permute-start.10) | collective-permute-done | bytes 1048608 | tf_op jit(solution)/shard_map/ppermute | solution.py:9
  464.2 2.0 collective-permute-start.11
  466.6 12.5 %collective-permute-done.11 = bf16[2,2,2,128,512]{4,3,1,2,0:T(8,128)(2,1)S(1)} collective-permute-done((bf16[2,2,2,128,512]{4,3,1,2,0:T(8,128)(2,1)S(1)}, bf16[2,2,2,128,512]{4,3,1,2,0:T(8,128)(2,1)S(1)}, u32[]{:S(2)}, u32[]{:S(2)}) %collective-permute-start.11) | collective-permute-done | bytes 1048608 | tf_op jit(solution)/shard_map/ppermute | solution.py:9
  480.5 17.3 %collective-permute-start.12 = (bf16[2,2,2,128,512]{4,3,1,2,0:T(8,128)(2,1)S(1)}, bf16[2,2,2,128,512]{4,3,1,2,0:T(8,128)(2,1)S(1)}, u32[]{:S(2)}, u32[]{:S(2)}) collective-permute-start(bf16[2,2,2,128,512]{4,3,1,2,0:T(8,128)(2,1)S(1)} %get-tuple-element.18), channel_id=1, source_target_pairs={{0,64},{16,80},{32,96},{48,112},{64,0},{80,16},{96,32},{112,48},{1... | collective-permute-start | bytes 3145736 | tf_op jit(solution)/shard_map/ppermute | solution.py:9
  498.3 12.4 %collective-permute-done.12 = bf16[2,2,2,128,512]{4,3,1,2,0:T(8,128)(2,1)S(1)} collective-permute-done((bf16[2,2,2,128,512]{4,3,1,2,0:T(8,128)(2,1)S(1)}, bf16[2,2,2,128,512]{4,3,1,2,0:T(8,128)(2,1)S(1)}, u32[]{:S(2)}, u32[]{:S(2)}) %collective-permute-start.12) | collective-permute-done | bytes 1048608 | tf_op jit(solution)/shard_map/ppermute | solution.py:9
  512.7 1.3 collective-permute-start.13
  514.0 5.8 collective-permute-done.13
  521.9 66.1 %all-gather.4.cloned.1.call-done = bf16[1024,1536]{0,1:T(8,128)(2,1)} async-done(((bf16[128,1536]{0,1:T(8,128)(2,1)}), bf16[1024,1536]{0,1:T(8,128)(2,1)}) %all-gather.4.cloned.1.call-update) | async-done | bytes 3145744 | tf_op jit(solution)/shard_map/all_gather | solution.py:176
  588.0 6.3 convolution_convert_fusion
  594.4 2.6 copy.148
  597.3 1.3 copy-done.8
  598.5 6.7 fusion
  605.2 11.6 %all-reduce.4.cloned.1.call-done = bf16[128,512]{1,0:T(8,128)(2,1)} async-done(((bf16[128,512]{1,0:T(8,128)(2,1)}), bf16[128,512]{1,0:T(8,128)(2,1)}) %all-reduce.4.cloned.1.call-update) | async-done | bytes 131088 | tf_op jit(solution)/shard_map/psum | solution.py:190
  616.8 1.6 convert_element_type.211
  618.5 35.2 %reduce-scatter.7.cloned.1.call-done = bf16[128,1024]{1,0:T(8,128)(2,1)} async-done(((bf16[1024,1024]{1,0:T(8,128)(2,1)}), bf16[128,1024]{1,0:T(8,128)(2,1)}) %reduce-scatter.7.cloned.1.call-update) | async-done | bytes 262160
  653.6 1.8 copy.149
  655.4 82.1 %all-gather.6.cloned.1.call-done = bf16[2048,1536]{0,1:T(8,128)(2,1)} async-done(((bf16[1024,1536]{0,1:T(8,128)(2,1)}), bf16[2048,1536]{0,1:T(8,128)(2,1)}) %all-gather.6.cloned.1.call-update) | async-done | bytes 6291472 | tf_op jit(solution)/shard_map/all_gather | solution.py:188
  737.5 11.1 %reshape.746 = bf16[2,1024,1536]{1,0,2:T(2,128)(2,1)} reshape(bf16[2048,1536]{0,1:T(8,128)(2,1)} %all-gather.6.cloned.1.call-done) | data formatting | bytes 12582912 | tf_op jit(solution)/shard_map/all_gather | solution.py:188
  748.6 18.2 %reduce_sum.12 = bf16[1024,1536]{0,1:T(8,128)(2,1)} reduce(bf16[2,1024,1536]{1,0,2:T(2,128)(2,1)} %reshape.746, bf16[]{:T(256)} %constant.275.clone.1), dimensions={0}, to_apply=%region_2.3 | reduce | flops 1572864 | bytes 9437186 | tf_op jit(solution)/shard_map/reduce_sum | solution.py:187
  766.8 4.6 copy.117
  (135 shorter events, 28.7 us)
Async XLA Ops:
  11.2 36.5 %all-to-all-start = ((bf16[128,8,1024]{0,2,1:T(8,128)(2,1)}), bf16[128,8,1024]{0,2,1:T(8,128)(2,1)S(1)}, u32[]{:S(2)}, u32[]{:S(2)}) async-start(bf16[128,8,1024]{0,2,1:T(8,128)(2,1)} %bitcast.321), calls=%async_computation | async-start | bytes 4194304 | tf_op jit(solution)/shard_map/all_to_all | solution.py:127
  19.3 135.9 %reduce-scatter.5.cloned.1.call-start = ((), (), s32[]{:S(2)}) async-start(), calls=%async_computation.3 | async-start | bytes 7077888 | tf_op jit(solution)/shard_map/reduce_scatter | solution.py:129
  59.0 0.7 copy-start.18
  59.0 529.0 %all-gather.4.cloned.1.call-start = ((), (), s32[]{:S(2)}) async-start(), calls=%async_computation.4 | async-start | bytes 3538944 | tf_op jit(solution)/shard_map/all_gather | solution.py:176
  155.9 4.3 collective-permute-start
  158.6 2.0 copy-start.11
  160.0 1.0 copy-start.10
  162.9 49.0 %collective-permute-start.1 = (f32[2,2,2,128,512]{4,3,1,2,0:T(8,128)}, f32[2,2,2,128,512]{4,3,1,2,0:T(8,128)}, u32[]{:S(2)}, u32[]{:S(2)}) collective-permute-start(f32[2,2,2,128,512]{4,3,1,2,0:T(8,128)} %pad_maximum_fusion), channel_id=1, source_target_pairs={{0,64},{16,80},{32,96},{48,112},{64,0},{80,16},{96,32},{112,48},{1... | collective-permute-start | bytes 6291464 | tf_op jit(solution)/shard_map/ppermute | solution.py:9
  214.3 4.5 copy-start
  214.3 4.5 copy-start.2
  218.8 45.3 %collective-permute-start.2 = (f32[2,2,2,128,512]{4,3,1,2,0:T(8,128)}, f32[2,2,2,128,512]{4,3,1,2,0:T(8,128)}, u32[]{:S(2)}, u32[]{:S(2)}) collective-permute-start(f32[2,2,2,128,512]{4,3,1,2,0:T(8,128)} %maximum_select_fusion), channel_id=1, source_target_pairs={{0,32},{16,48},{32,0},{48,16},{64,96},{80,112},{96,64},{112,80},{1... | collective-permute-start | bytes 6291464 | tf_op jit(solution)/shard_map/ppermute | solution.py:9
  267.9 1.2 copy-start.1
  267.9 1.5 copy-start.3
  274.3 46.0 %collective-permute-start.3 = (f32[2,2,2,128,512]{4,3,1,2,0:T(8,128)}, f32[2,2,2,128,512]{4,3,1,2,0:T(8,128)S(1)}, u32[]{:S(2)}, u32[]{:S(2)}) collective-permute-start(f32[2,2,2,128,512]{4,3,1,2,0:T(8,128)} %maximum_select_fusion.1), channel_id=1, source_target_pairs={{0,16},{16,0},{32,48},{48,32},{64,80},{80,64},{96,112},{112,96},{1... | collective-permute-start | bytes 6291464 | tf_op jit(solution)/shard_map/ppermute | solution.py:9
  276.6 48.3 %copy-start.13 = (f32[2,128]{1,0:T(2,128)}, f32[2,128]{1,0:T(2,128)S(1)}, u32[]{:S(2)}) copy-start(f32[2,128]{1,0:T(2,128)S(1)} %get-tuple-element.90) | copy-start | bytes 3076
  276.6 48.3 %copy-start.15 = (f32[2,128]{1,0:T(2,128)}, f32[2,128]{1,0:T(2,128)S(1)}, u32[]{:S(2)}) copy-start(f32[2,128]{1,0:T(2,128)S(1)} %get-tuple-element.91) | copy-start | bytes 3076
  276.6 59.7 %copy-start.19 = (f32[2,128]{1,0:T(2,128)}, f32[2,128]{1,0:T(2,128)S(1)}, u32[]{:S(2)}) copy-start(f32[2,128]{1,0:T(2,128)S(1)} %get-tuple-element.88) | copy-start | bytes 3076
  276.7 59.7 %copy-start.21 = (f32[2,128]{1,0:T(2,128)}, f32[2,128]{1,0:T(2,128)S(1)}, u32[]{:S(2)}) copy-start(f32[2,128]{1,0:T(2,128)S(1)} %get-tuple-element.89) | copy-start | bytes 3076
  331.1 2.1 copy-start.4
  333.1 1.0 copy-start.6
  337.5 11.0 %collective-permute-start.4 = (bf16[2,1,2,128,512]{4,3,2,1,0:T(8,128)(2,1)S(1)}, bf16[2,1,2,128,512]{4,3,2,1,0:T(8,128)(2,1)S(1)}, u32[]{:S(2)}, u32[]{:S(2)}) collective-permute-start(bf16[2,1,2,128,512]{4,3,2,1,0:T(8,128)(2,1)S(1)} %fusion.33), channel_id=1, source_target_pairs={{0,16},{16,0},{32,48},{48,32},{64,80},{80,64},{96,112},{112,96},{1... | collective-permute-start | bytes 1572872 | tf_op jit(solution)/shard_map/ppermute | solution.py:9
  349.2 10.8 %collective-permute-start.5 = (bf16[2,1,2,128,512]{4,3,2,1,0:T(8,128)(2,1)S(1)}, bf16[2,1,2,128,512]{4,3,2,1,0:T(8,128)(2,1)S(1)}, u32[]{:S(2)}, u32[]{:S(2)}) collective-permute-start(bf16[2,1,2,128,512]{4,3,2,1,0:T(8,128)(2,1)S(1)} %get-tuple-element.27), channel_id=1, source_target_pairs={{0,32},{16,48},{32,0},{48,16},{64,96},{80,112},{96,64},{112,80},{1... | collective-permute-start | bytes 1572872 | tf_op jit(solution)/shard_map/ppermute | solution.py:9
  360.2 2.4 copy-start.9
  361.5 12.2 %collective-permute-start.6 = (bf16[2,1,2,128,512]{4,3,2,1,0:T(8,128)(2,1)}, bf16[2,1,2,128,512]{4,3,2,1,0:T(8,128)(2,1)S(1)}, u32[]{:S(2)}, u32[]{:S(2)}) collective-permute-start(bf16[2,1,2,128,512]{4,3,2,1,0:T(8,128)(2,1)} %get-tuple-element.25), channel_id=1, source_target_pairs={{0,64},{16,80},{32,96},{48,112},{64,0},{80,16},{96,32},{112,48},{1... | collective-permute-start | bytes 1572872 | tf_op jit(solution)/shard_map/ppermute | solution.py:9
  374.4 0.7 copy-start.17
  376.2 23.0 %collective-permute-start.7 = (f32[2,1,2,128,512]{4,3,2,1,0:T(8,128)S(1)}, f32[2,1,2,128,512]{4,3,2,1,0:T(8,128)S(1)}, u32[]{:S(2)}, u32[]{:S(2)}) collective-permute-start(f32[2,1,2,128,512]{4,3,2,1,0:T(8,128)S(1)} %pad_maximum_fusion.3), channel_id=1, source_target_pairs={{0,64},{16,80},{32,96},{48,112},{64,0},{80,16},{96,32},{112,48},{1... | collective-permute-start | bytes 3145736 | tf_op jit(solution)/shard_map/ppermute | solution.py:9
  400.0 15.8 %collective-permute-start.8 = (f32[2,1,2,128,512]{4,3,2,1,0:T(8,128)S(1)}, f32[2,1,2,128,512]{4,3,2,1,0:T(8,128)S(1)}, u32[]{:S(2)}, u32[]{:S(2)}) collective-permute-start(f32[2,1,2,128,512]{4,3,2,1,0:T(8,128)S(1)} %maximum_select_fusion.3), channel_id=1, source_target_pairs={{0,32},{16,48},{32,0},{48,16},{64,96},{80,112},{96,64},{112,80},{1... | collective-permute-start | bytes 3145736 | tf_op jit(solution)/shard_map/ppermute | solution.py:9
  417.2 16.9 %collective-permute-start.9 = (f32[2,1,2,128,512]{4,3,2,1,0:T(8,128)S(1)}, f32[2,1,2,128,512]{4,3,2,1,0:T(8,128)S(1)}, u32[]{:S(2)}, u32[]{:S(2)}) collective-permute-start(f32[2,1,2,128,512]{4,3,2,1,0:T(8,128)S(1)} %maximum_select_fusion.4), channel_id=1, source_target_pairs={{0,16},{16,0},{32,48},{48,32},{64,80},{80,64},{96,112},{112,96},{1... | collective-permute-start | bytes 3145736 | tf_op jit(solution)/shard_map/ppermute | solution.py:9
  434.5 0.7 copy-start.14
  434.5 0.7 copy-start.16
  435.2 3.6 copy-start.5
  435.2 3.6 copy-start.7
  443.0 1.3 copy-start.20
  443.0 1.3 copy-start.22
  446.1 16.6 %collective-permute-start.10 = (bf16[2,2,2,128,512]{4,3,1,2,0:T(8,128)(2,1)S(1)}, bf16[2,2,2,128,512]{4,3,1,2,0:T(8,128)(2,1)S(1)}, u32[]{:S(2)}, u32[]{:S(2)}) collective-permute-start(bf16[2,2,2,128,512]{4,3,1,2,0:T(8,128)(2,1)S(1)} %fusion.4), channel_id=1, source_target_pairs={{0,16},{16,0},{32,48},{48,32},{64,80},{80,64},{96,112},{112,96},{1... | collective-permute-start | bytes 3145736 | tf_op jit(solution)/shard_map/ppermute | solution.py:9
  464.2 14.9 %collective-permute-start.11 = (bf16[2,2,2,128,512]{4,3,1,2,0:T(8,128)(2,1)S(1)}, bf16[2,2,2,128,512]{4,3,1,2,0:T(8,128)(2,1)S(1)}, u32[]{:S(2)}, u32[]{:S(2)}) collective-permute-start(bf16[2,2,2,128,512]{4,3,1,2,0:T(8,128)(2,1)S(1)} %get-tuple-element.20), channel_id=1, source_target_pairs={{0,32},{16,48},{32,0},{48,16},{64,96},{80,112},{96,64},{112,80},{1... | collective-permute-start | bytes 3145736 | tf_op jit(solution)/shard_map/ppermute | solution.py:9
  480.5 30.1 %collective-permute-start.12 = (bf16[2,2,2,128,512]{4,3,1,2,0:T(8,128)(2,1)S(1)}, bf16[2,2,2,128,512]{4,3,1,2,0:T(8,128)(2,1)S(1)}, u32[]{:S(2)}, u32[]{:S(2)}) collective-permute-start(bf16[2,2,2,128,512]{4,3,1,2,0:T(8,128)(2,1)S(1)} %get-tuple-element.18), channel_id=1, source_target_pairs={{0,64},{16,80},{32,96},{48,112},{64,0},{80,16},{96,32},{112,48},{1... | collective-permute-start | bytes 3145736 | tf_op jit(solution)/shard_map/ppermute | solution.py:9
  512.5 7.4 copy-start.12
  512.7 7.1 collective-permute-start.13
  521.1 95.7 %all-reduce.4.cloned.1.call-start = ((), (), s32[]{:S(2)}) async-start(), calls=%async_computation.5 | async-start | bytes 262144 | tf_op jit(solution)/shard_map/psum | solution.py:190
  521.9 131.8 %reduce-scatter.7.cloned.1.call-start = ((), (), s32[]{:S(2)}) async-start(), calls=%async_computation.7 | async-start | bytes 2359296
  596.9 1.6 copy-start.8
  597.0 140.5 %all-gather.6.cloned.1.call-start = ((), (), s32[]{:S(2)}) async-start(), calls=%async_computation.6 | async-start | bytes 9437184 | tf_op jit(solution)/shard_map/all_gather | solution.py:188
Sparse Core Ops, SparseCore 0:
  59.1 95.9 reduce-scatter.4
  521.3 66.7 all-gather.3
  591.0 25.7 all-reduce.3
  619.1 34.5 reduce-scatter.6
  655.7 81.7 all-gather.5
